TPU v7x, 512 devices: a whole 4x8x8 slice. The times are simulated.
512 devices in a mesh: frame: 4 (over x), vox: 128 (over y, z, core).
Axes of the slice: x: 4, y: 8, z: 8, core: 2. Of those that a mesh axis runs over, the one named last changes fastest.
Arguments:
- volume: float32 [4, 256, 512, 128], P('frame', 'vox'), may hold values from -60 to 60
Outputs:
- factor: float32 [256, 256], replicated
All inputs are finite; a program needn't handle non-finite values.
Results may differ from a plain program's by a relative error of at most 0.0001.
Values sent between devices are 32-bit elements; how exact they have to be, the bound alone decides.
No kernel may reach another device: no remote copies, remote signals or barrier semaphores. Data moves between devices by JAX's collectives and lax.ppermute only.
A program may use at most 64 MiB of HBM per device.

v0:
```python
import jax
import jax.numpy as jnp
from jax import lax
from jax.sharding import Mesh
from jax.sharding import PartitionSpec as P

VOX = ("vox_0", "vox_1", "vox_2")


def from_everyone(x, axis):
    copies = jnp.broadcast_to(x, (lax.axis_size(axis), *x.shape))
    return lax.all_to_all(copies, axis, split_axis=0, concat_axis=0, tiled=True)


def taken_together(x, axis):
    everything = from_everyone(x, axis)
    return jnp.sum(everything, axis=0)


def rows_for(lines, count):
    spare = -lines.shape[0] % count
    if not spare:
        return lines
    return jnp.concatenate([lines, jnp.zeros((spare, *lines.shape[1:]), lines.dtype)])


def joined_along(tiles, dim):
    lengths = list(tiles.shape[1:])
    lengths[dim] *= tiles.shape[0]
    return jnp.moveaxis(tiles, 0, dim).reshape(lengths)


def gather_axes(x, axes, dim):
    far, near = axes
    tiles = from_everyone(from_everyone(x, far), near)
    return joined_along(tiles.swapaxes(0, 1).reshape(-1, *x.shape), dim)


def split_up(x, dim, count):
    before, after = (x.shape[:dim], x.shape[dim + 1 :])
    return jnp.moveaxis(x.reshape(*before, count, -1, *after), dim, 0)


def summed_on_arrival(x, axis, dim):
    count = lax.axis_size(axis)
    tiles = lax.all_to_all(split_up(x, dim, count), axis, 0, 0, tiled=True)
    return jnp.sum(tiles, axis=0)


def summed_rows(x, axes, dim):
    far, near = axes
    tiles = split_up(x, dim, lax.axis_size(far))
    nearer = summed_on_arrival(tiles, near, dim + 1)
    arrived = lax.all_to_all(nearer, far, split_axis=0, concat_axis=0, tiled=True)
    return arrived.sum(axis=0)


def nested_sum(x, axes):
    lines = x.reshape(-1, x.shape[-1])
    padded = rows_for(lines, lax.axis_size(axes[0]) * lax.axis_size(axes[1]))
    whole = gather_axes(summed_rows(padded, axes, 0), axes, 0)
    return lax.slice_in_dim(whole, 0, len(lines)).reshape(x.shape)


def block_gram(block, scale):
    rows_z = block.shape[1]
    column_block = jnp.moveaxis(block, 1, 0).reshape(rows_z, -1)
    return jnp.dot(
        column_block,
        column_block.T,
        precision=lax.Precision.HIGHEST,
        preferred_element_type=jnp.float32,
    ) / jnp.float32(scale)


def per_device(volume):
    column_total = float(
        volume.shape[0] * lax.axis_size("frame") * volume.shape[2] * volume.shape[3]
    )
    regrouped = lax.all_to_all(volume, VOX, split_axis=2, concat_axis=1, tiled=True)
    local_gram = taken_together(block_gram(regrouped, column_total), "frame")
    gram_all = nested_sum(local_gram, (("vox_0", "vox_1"), "vox_2"))
    factor = jnp.linalg.cholesky(gram_all)
    return factor


def solution(mesh):
    finer = Mesh(
        mesh.devices.reshape(mesh.shape["frame"], 8, 8, 2), ("frame", "vox_0", "vox_1", "vox_2")
    )
    in_specs = (P("frame", VOX, None, None),)
    out_specs = P()
    return jax.shard_map(
        per_device, mesh=finer, in_specs=in_specs, out_specs=out_specs, check_vma=False
    )
```

profile of v0, /device:TPU:1, one launch (start us, length us, event | category | flops | bytes accessed | tf_op | source)
XLA Modules:
  0.0 140.0 jit_solution(2922442329392517590)
XLA Ops:
  0.0 1.4 %copy.19 = f32[1,2,512,128]{3,1,0,2:T(2,128)S(1)} copy(f32[1,2,512,128]{3,2,1,0:T(8,128)} %param.1) | data formatting | bytes 1048576 | tf_op args[0]
  1.4 37.6 %all_to_all.40 = f32[1,2,512,128]{3,1,0,2:T(2,128)S(1)} all-to-all(f32[1,2,512,128]{3,1,0,2:T(2,128)S(1)} %copy.19), channel_id=1, replica_groups=mesh['frame'=4,'vox_0'=8,'vox_1'=8,'vox_2'=2] {'vox_0','vox_1','vox_2'}, dimensions={2} | all-to-all | bytes 1048576 | tf_op jit(solution)/shard_map/all_to_all | solution.py:80
  39.1 0.1 copy.20
  39.2 0.6 convolution_multiply_fusion
  39.8 0.1 broadcast_in_dim.11
  39.9 16.6 %all_to_all.41 = f32[4,256,256]{2,1,0:T(8,128)S(1)} all-to-all(f32[4,256,256]{2,1,0:T(8,128)S(1)} %broadcast_in_dim.11), channel_id=1, replica_groups=mesh['frame'=4,'vox_0'=8,'vox_1'=8,'vox_2'=2] {'frame'}, dimensions={0} | all-to-all | bytes 2097152 | tf_op jit(solution)/shard_map/all_to_all | solution.py:12
  56.6 0.1 reduce_sum.27
  56.7 0.1 reshape_reshape.6
  56.9 6.8 %all_to_all.42 = f32[2,64,2,256]{3,2,1,0:T(2,128)S(1)} all-to-all(f32[2,64,2,256]{3,2,1,0:T(2,128)S(1)} %copy.21), channel_id=1, replica_groups=mesh['frame'=4,'vox_0'=8,'vox_1'=8,'vox_2'=2] {'vox_2'}, dimensions={0} | all-to-all | bytes 524288 | tf_op jit(solution)/shard_map/all_to_all | solution.py:46
  63.7 0.2 reduce_sum.28
  63.9 16.6 %all_to_all.43 = f32[64,2,256]{2,1,0:T(2,128)S(1)} all-to-all(f32[64,2,256]{2,1,0:T(2,128)S(1)} %reduce_sum.28), channel_id=1, replica_groups=mesh['frame'=4,'vox_0'=8,'vox_1'=8,'vox_2'=2] {'vox_0','vox_1'}, dimensions={0} | all-to-all | bytes 262144 | tf_op jit(solution)/shard_map/all_to_all | solution.py:54
  80.5 0.1 reduce_sum.29
  80.6 15.6 %all_to_all.44 = f32[64,2,256]{2,1,0:T(2,128)S(1)} all-to-all(f32[64,2,256]{2,1,0:T(2,128)S(1)} %broadcast_in_dim.12), channel_id=1, replica_groups=mesh['frame'=4,'vox_0'=8,'vox_1'=8,'vox_2'=2] {'vox_0','vox_1'}, dimensions={0} | all-to-all | bytes 262144 | tf_op jit(solution)/shard_map/all_to_all | solution.py:12
  96.2 0.1 broadcast_in_dim.13
  96.3 6.7 %all_to_all.45 = f32[2,64,2,256]{3,2,1,0:T(2,128)S(1)} all-to-all(f32[2,64,2,256]{3,2,1,0:T(2,128)S(1)} %broadcast_in_dim.13), channel_id=1, replica_groups=mesh['frame'=4,'vox_0'=8,'vox_1'=8,'vox_2'=2] {'vox_2'}, dimensions={0} | all-to-all | bytes 524288 | tf_op jit(solution)/shard_map/all_to_all | solution.py:12
  103.0 0.2 reshape_reshape.7
  103.2 0.1 copy.24
  103.4 11.7 %cholesky.50 = f32[128,128]{1,0:T(8,128)S(1)} custom-call(f32[128,128]{1,0:T(8,128)S(1)} %cholesky.118), custom_call_target="Cholesky" | custom-call | tf_op jit(solution)/shard_map/jit(cholesky)/cholesky | solution.py:83
  115.2 9.8 %custom-call.11 = f32[1,128,128]{1,2,0:T(8,128)S(1)} custom-call(f32[1,128,128]{2,1,0:T(8,128)S(1)} %get-tuple-element.8), custom_call_target="InvertDiagBlocksLowerTriangular" | custom-call | tf_op jit(solution)/shard_map/jit(cholesky)/cholesky | solution.py:83
  125.0 0.2 constant_dynamic-update-slice_fusion.1
  125.2 0.3 convolution_subtract_fusion
  125.5 11.7 %cholesky.105 = f32[128,128]{1,0:T(8,128)S(1)} custom-call(f32[128,128]{1,0:T(8,128)S(1)} %convolution_subtract_fusion), custom_call_target="Cholesky" | custom-call | tf_op jit(solution)/shard_map/jit(cholesky)/cholesky | solution.py:83
  137.2 0.7 compare_reduce_fusion
  139.3 0.7 select_select_fusion
  (8 shorter events, 0.3 us)
where the time goes:
time: 140 us
  blocking collectives  100 us (71%)
  other arithmetic  35.1 us (25%)
  local copies, waits for them, and re-layouts  2.34 us (2%)
  between operations  1.46 us (1%)
    all_to_all x3, blocking collectives, from_everyone(): return lax.all_to_all(copies, axis, split_axis=0, concat_axis=0, tiled=True)  38.9 us
    all_to_all x1, blocking collectives, per_device(): lax.all_to_all(volume, VOX, split_axis=2, concat_axis=1, tiled=True)  37.6 us
    another operation x6, other arithmetic, per_device(): factor = jnp.linalg.cholesky(gram_all)  34 us
    all_to_all x1, blocking collectives, summed_rows(): lax.all_to_all(nearer, far, split_axis=0, concat_axis=0, tiled=True)  16.6 us
    all_to_all x1, blocking collectives, summed_on_arrival(): tiles = lax.all_to_all(split_up(x, dim, count), axis, 0, 0, tiled=True)  6.8 us

commit v1 on v0

v1 whole, which is shorter than its diff:
```python
import jax
import jax.numpy as jnp
from jax import lax
from jax.experimental import pallas as pl
from jax.experimental.pallas import tpu as pltpu
from jax.sharding import Mesh
from jax.sharding import PartitionSpec as P

VOX = ("vox_0", "vox_1", "vox_2")
PAIR = ("frame", "vox_2")


def exchange(tiles, axes):
    return lax.all_to_all(tiles, axes, split_axis=0, concat_axis=0, tiled=True)


def from_everyone(x, axes):
    return exchange(jnp.broadcast_to(x, (lax.axis_size(axes), *x.shape)), axes)


def eye_parts(half):
    rows = lax.broadcasted_iota(jnp.int32, (half, half), 0)
    cols = lax.broadcasted_iota(jnp.int32, (half, half), 1)
    return rows, cols


def folded_gram_body(scale, half, x_ref, out_ref):
    total = jnp.zeros((2 * half, 2 * half), jnp.float32)
    for line in range(x_ref.shape[1]):
        rows_z = x_ref[:, line, :]
        total += lax.dot_general(
            rows_z,
            rows_z,
            (((1,), (1,)), ((), ())),
            precision=lax.Precision.HIGHEST,
            preferred_element_type=jnp.float32,
        )
    total = total * scale
    rows, cols = eye_parts(half)
    low = total[half:, half:]
    out_ref[0:half, :] = jnp.where(rows >= cols, total[:half, :half], low)
    out_ref[half : 2 * half, :] = total[half:, :half]
    spare = out_ref.shape[0] - 2 * half
    diagonal = jnp.sum(jnp.where(rows == cols, low, 0.0), axis=0, keepdims=True)
    out_ref[2 * half :, :] = jnp.broadcast_to(diagonal, (spare, half))


def folded_gram(columns, column_total, padded):
    rows_z = columns.shape[0]
    half = rows_z // 2

    def body(x_ref, out_ref):
        folded_gram_body(1.0 / column_total, half, x_ref, out_ref)

    return pl.pallas_call(
        body,
        out_shape=jax.ShapeDtypeStruct((padded, half), jnp.float32),
        name="folded_gram",
    )(columns)


def per_device(volume):
    _, rows_z, lines, width = volume.shape
    voxes = lax.axis_size(VOX)
    half = rows_z * voxes // 2
    column_total = float(lax.axis_size("frame") * lines * width)
    tiles = volume.reshape(rows_z, voxes, lines // voxes, width).swapaxes(0, 1)
    columns = exchange(tiles, VOX).reshape(2 * half, lines // voxes, width)
    pair = lax.axis_size(PAIR)
    share = -(-(2 * half + 1) // (8 * pair)) * 8
    folded = folded_gram(columns, column_total, share * pair)
    part = jnp.sum(exchange(folded.reshape(pair, share, half), PAIR), axis=0)
    part = jnp.sum(from_everyone(part, "vox_0"), axis=0)
    part = jnp.sum(from_everyone(part, "vox_1"), axis=0)
    whole = from_everyone(part, PAIR).reshape(pair * share, half)
    rows, cols = eye_parts(half)
    top = jnp.tril(whole[:half])
    low = jnp.where(rows > cols, whole[:half].T, 0.0)
    low = low + jnp.where(rows == cols, whole[2 * half], 0.0)
    gram = jnp.concatenate(
        [
            jnp.concatenate([top, jnp.zeros_like(top)], axis=1),
            jnp.concatenate([whole[half : 2 * half], low], axis=1),
        ]
    )
    return jnp.tril(lax.linalg.cholesky(gram, symmetrize_input=False))


def solution(mesh):
    finer = Mesh(
        mesh.devices.reshape(mesh.shape["frame"], 8, 8, 2), ("frame", "vox_0", "vox_1", "vox_2")
    )
    return jax.shard_map(
        per_device,
        mesh=finer,
        in_specs=(P("frame", VOX, None, None),),
        out_specs=P(),
        check_vma=False,
    )
```

time: 140 us -> 124 us (0.89)
  blocking collectives: 100 us -> 82.5 us
  Pallas kernels: 0 us -> 2.88 us
    all_to_all x6 -> x5, blocking collectives: 100 us -> 82.5 us  [exchange(): return lax.all_to_all(tiles, axes, split_axis=0, concat_axis=0, tiled=True)]
    pallas_call x0 -> x1, Pallas kernels: none -> 2.88 us  [folded_gram(): pl.pallas_call(body, out_shape=jax.ShapeDtypeStruct((padded, half), jnp.f...]
    unnamed x1 -> x0, local copies, waits for them, and re-layouts: 1.45 us -> none
where the time goes in v1:
time: 124 us; the launch traced here: 123 us
  blocking collectives  82.5 us (67%)
  other arithmetic  34.8 us (28%)
  Pallas kernels  2.88 us (2%)
  between operations  1.43 us (1%)
  local copies, waits for them, and re-layouts  1.28 us (1%)
    all_to_all x5, blocking collectives, exchange(): return lax.all_to_all(tiles, axes, split_axis=0, concat_axis=0, tiled=True)  82.5 us
    another operation x6, other arithmetic, per_device(): return jnp.tril(lax.linalg.cholesky(gram, symmetrize_input=False))  34 us
    pallas_call x1, Pallas kernels, folded_gram(): pl.pallas_call(body, out_shape=jax.ShapeDtypeStruct((padded, half), jnp.f...  2.88 us

profile of v1, /device:TPU:1, one launch (start us, length us, event | category | flops | bytes accessed | tf_op | source)
XLA Modules:
  0.0 123.4 jit_solution(18380468556200019957)
XLA Ops:
  0.0 1.1 copy.15
  1.1 37.7 %all_to_all.25 = f32[128,2,4,128]{3,2,1,0:T(4,128)} all-to-all(f32[128,2,4,128]{3,2,1,0:T(4,128)S(1)} %bitcast.21), channel_id=1, replica_groups=mesh['frame'=4,'vox_0'=8,'vox_1'=8,'vox_2'=2] {'vox_0','vox_1','vox_2'}, dimensions={0} | all-to-all | bytes 1048576 | tf_op jit(solution)/shard_map/all_to_all | solution.py:14
  38.9 2.9 %folded_gram.1 = f32[320,128]{1,0:T(8,128)} custom-call(f32[256,4,128]{2,1,0:T(4,128)} %bitcast.20), custom_call_target="tpu_custom_call" | custom-call | tf_op jit(solution)/shard_map/folded_gram/pallas_call | solution.py:55
  41.7 11.9 %all_to_all.26 = f32[8,40,128]{2,1,0:T(8,128)S(1)} all-to-all(f32[8,40,128]{2,1,0:T(8,128)} %bitcast.26), channel_id=1, replica_groups=mesh['frame'=4,'vox_0'=8,'vox_1'=8,'vox_2'=2] {'frame','vox_2'}, dimensions={0} | all-to-all | bytes 327680 | tf_op jit(solution)/shard_map/all_to_all | solution.py:14
  53.7 10.7 %all_to_all.27 = f32[8,40,128]{2,1,0:T(8,128)S(1)} all-to-all(f32[8,40,128]{2,1,0:T(8,128)S(1)} %broadcast_in_dim.25), channel_id=1, replica_groups=mesh['frame'=4,'vox_0'=8,'vox_1'=8,'vox_2'=2] {'vox_0'}, dimensions={0} | all-to-all | bytes 327680 | tf_op jit(solution)/shard_map/all_to_all | solution.py:14
  64.4 10.8 %all_to_all.28 = f32[8,40,128]{2,1,0:T(8,128)S(1)} all-to-all(f32[8,40,128]{2,1,0:T(8,128)S(1)} %broadcast_in_dim.26), channel_id=1, replica_groups=mesh['frame'=4,'vox_0'=8,'vox_1'=8,'vox_2'=2] {'vox_1'}, dimensions={0} | all-to-all | bytes 327680 | tf_op jit(solution)/shard_map/all_to_all | solution.py:14
  75.2 11.4 %all_to_all.29 = f32[8,40,128]{2,1,0:T(8,128)S(1)} all-to-all(f32[8,40,128]{2,1,0:T(8,128)S(1)} %broadcast_in_dim.27), channel_id=1, replica_groups=mesh['frame'=4,'vox_0'=8,'vox_1'=8,'vox_2'=2] {'frame','vox_2'}, dimensions={0} | all-to-all | bytes 327680 | tf_op jit(solution)/shard_map/all_to_all | solution.py:14
  86.7 11.7 %cholesky.49 = f32[128,128]{1,0:T(8,128)S(1)} custom-call(f32[128,128]{1,0:T(8,128)S(1)} %fusion.3), custom_call_target="Cholesky" | custom-call | tf_op jit(solution)/shard_map/cholesky | solution.py:86
  98.5 0.1 copy.7
  98.6 9.8 %custom-call.8 = f32[1,128,128]{1,2,0:T(8,128)S(1)} custom-call(f32[1,128,128]{2,1,0:T(8,128)S(1)} %get-tuple-element.8), custom_call_target="InvertDiagBlocksLowerTriangular" | custom-call | tf_op jit(solution)/shard_map/cholesky | solution.py:86
  108.4 0.2 constant_dynamic-update-slice_fusion.1
  108.6 0.3 convolution_subtract_fusion
  108.9 11.7 %cholesky.98 = f32[128,128]{1,0:T(8,128)S(1)} custom-call(f32[128,128]{1,0:T(8,128)S(1)} %convolution_subtract_fusion), custom_call_target="Cholesky" | custom-call | tf_op jit(solution)/shard_map/cholesky | solution.py:86
  120.6 0.7 compare_reduce_fusion
  122.7 0.7 select_select_fusion
  (12 shorter events, 0.2 us)

commit v2 on v1

--- a/solution.py
+++ b/solution.py
@@ -8,6 +8,8 @@
 
 VOX = ("vox_0", "vox_1", "vox_2")
 PAIR = ("frame", "vox_2")
+LANES = 128
+SUBS = 8
 
 
 def exchange(tiles, axes):
@@ -39,7 +41,7 @@
     rows, cols = eye_parts(half)
     low = total[half:, half:]
     out_ref[0:half, :] = jnp.where(rows >= cols, total[:half, :half], low)
-    out_ref[half : 2 * half, :] = total[half:, :half]
+    out_ref[half : 2 * half, :] = total[:half, half:]
     spare = out_ref.shape[0] - 2 * half
     diagonal = jnp.sum(jnp.where(rows == cols, low, 0.0), axis=0, keepdims=True)
     out_ref[2 * half :, :] = jnp.broadcast_to(diagonal, (spare, half))
@@ -59,6 +61,90 @@
     )(columns)
 
 
+def row_of(x, k):
+    return jnp.broadcast_to(x[k : k + 1, :], x.shape)
+
+def lane_of(x, k):
+    return jnp.broadcast_to(x[:, k : k + 1], (x.shape[0], LANES))
+
+def factor_half(work, poison):
+    width = work.shape[1]
+    slabs = [slice(s, s + LANES) for s in range(0, width, LANES)]
+    panels = LANES // SUBS
+    sub = lax.broadcasted_iota(jnp.int32, (SUBS, LANES), 0)
+
+    def rows(i):
+        return slice(i * SUBS, (i + 1) * SUBS)
+
+    current = [work[rows(0), s] for s in slabs]
+    for j in range(panels):
+        here = [lane_of(current[0], j * SUBS + k) for k in range(SUBS)]
+        more = j + 1 < panels
+        if more:
+            ahead = [work[rows(j + 1), s] for s in slabs]
+            below = [lane_of(ahead[0], j * SUBS + k) for k in range(SUBS)]
+        done = [jnp.zeros((SUBS, LANES), jnp.float32) for _ in slabs]
+        lines = []
+        for k in range(SUBS):
+            inverse = lax.rsqrt(row_of(here[k], k))
+            poison = poison + inverse * 0.0
+            column = here[k] * inverse
+            line = [row_of(c, k) * inverse for c in current]
+            lines.append(line)
+            if more:
+                lower = below[k] * inverse
+                ahead = [a - lower * y for a, y in zip(ahead, line)]
+            for l in range(k + 1, SUBS):
+                pick = row_of(column, l)
+                here[l] = here[l] - column * pick
+                if more:
+                    below[l] = below[l] - lower * pick
+            if k + 1 < SUBS:
+                current = [c - column * y for c, y in zip(current, line)]
+            done = [jnp.where(sub == k, y, d) for y, d in zip(line, done)]
+        for s, d in zip(slabs, done):
+            work[rows(j), s] = d
+        if j + 2 < panels:
+            turned = done[0].T
+            for i in range(j + 2, panels):
+                tile = turned[rows(i), :]
+                value = [work[rows(i), s] for s in slabs]
+                for k in range(SUBS):
+                    factor = lane_of(tile, k)
+                    value = [v - factor * y for v, y in zip(value, lines[k])]
+                for s, v in zip(slabs, value):
+                    work[rows(i), s] = v
+        if more:
+            current = ahead
+    return poison
+
+def factor_body(half, x_ref, out_ref, first, second):
+    r = lax.broadcasted_iota(jnp.int32, (half, half), 0)
+    c = lax.broadcasted_iota(jnp.int32, (half, half), 1)
+    folded = x_ref[0:half, :]
+    turned = folded.T
+    first[:, 0:half] = jnp.where(r >= c, folded, turned)
+    first[:, half:] = x_ref[half : 2 * half, :]
+    second[...] = jnp.where(r == c, x_ref[2 * half : 2 * half + 1, :], jnp.where(r < c, folded, turned))
+    poison = factor_half(first, jnp.zeros((SUBS, LANES), jnp.float32))
+    across = first[:, half:]
+    second[...] -= lax.dot_general(across, across, (((0,), (0,)), ((), ())), precision=lax.Precision.HIGHEST, preferred_element_type=jnp.float32)
+    out_ref[0:half, half:] = jnp.zeros((half, half), jnp.float32)
+    poison = factor_half(second, poison)
+    spoil = poison[0:1, :]
+    out_ref[half:, 0:half] = across.T + spoil
+    out_ref[0:half, 0:half] = jnp.where(r >= c, first[:, 0:half].T + spoil, 0.0)
+    out_ref[half:, half:] = jnp.where(r >= c, second[...].T + spoil, 0.0)
+
+def factor(whole, half):
+    return pl.pallas_call(
+        lambda *refs: factor_body(half, *refs),
+        out_shape=jax.ShapeDtypeStruct((2 * half, 2 * half), jnp.float32),
+        scratch_shapes=[pltpu.VMEM((half, 2 * half), jnp.float32), pltpu.VMEM((half, half), jnp.float32)],
+        name="factor",
+    )(whole)
+
+
 def per_device(volume):
     _, rows_z, lines, width = volume.shape
     voxes = lax.axis_size(VOX)
@@ -73,17 +159,7 @@
     part = jnp.sum(from_everyone(part, "vox_0"), axis=0)
     part = jnp.sum(from_everyone(part, "vox_1"), axis=0)
     whole = from_everyone(part, PAIR).reshape(pair * share, half)
-    rows, cols = eye_parts(half)
-    top = jnp.tril(whole[:half])
-    low = jnp.where(rows > cols, whole[:half].T, 0.0)
-    low = low + jnp.where(rows == cols, whole[2 * half], 0.0)
-    gram = jnp.concatenate(
-        [
-            jnp.concatenate([top, jnp.zeros_like(top)], axis=1),
-            jnp.concatenate([whole[half : 2 * half], low], axis=1),
-        ]
-    )
-    return jnp.tril(lax.linalg.cholesky(gram, symmetrize_input=False))
+    return factor(whole, half)
 
 
 def solution(mesh):

time: 124 us -> 99 us (0.80)
  other arithmetic: 34.8 us -> 0.04 us
  Pallas kernels: 2.88 us -> 14.1 us
  between operations: 1.43 us -> 0.04 us
    another operation x6 -> x0, other arithmetic: 34 us -> none  [per_device(): return jnp.tril(lax.linalg.cholesky(gram, symmetrize_input=False))]
    pallas_call x0 -> x1, Pallas kernels: none -> 11.2 us  [factor(): pl.pallas_call(lambda *refs: factor_body(half, *refs), out_shape=jax.Shap...]
where the time goes in v2:
time: 99 us; the launch traced here: 98.5 us
  blocking collectives  83.2 us (84%)
  Pallas kernels  14.1 us (14%)
  local copies, waits for them, and re-layouts  1.17 us (1%)
    all_to_all x5, blocking collectives, exchange(): return lax.all_to_all(tiles, axes, split_axis=0, concat_axis=0, tiled=True)  83.2 us
    pallas_call x1, Pallas kernels, factor(): pl.pallas_call(lambda *refs: factor_body(half, *refs), out_shape=jax.Shap...  11.2 us
    pallas_call x1, Pallas kernels, folded_gram(): pl.pallas_call(body, out_shape=jax.ShapeDtypeStruct((padded, half), jnp.f...  2.88 us

profile of v2, /device:TPU:1, one launch (start us, length us, event | category | flops | bytes accessed | tf_op | source)
XLA Modules:
  0.0 98.5 jit_solution(16770429717327264900)
XLA Ops:
  0.0 1.1 %copy.5 = f32[2,128,4,128]{3,2,0,1:T(4,128)S(1)} copy(f32[2,128,4,128]{3,2,1,0:T(4,128)} %bitcast.11) | data formatting | bytes 1048576 | tf_op jit(solution)/shard_map/reshape | solution.py:153
  1.1 37.7 %all_to_all.25 = f32[128,2,4,128]{3,2,1,0:T(4,128)} all-to-all(f32[128,2,4,128]{3,2,1,0:T(4,128)S(1)} %bitcast.8), channel_id=1, replica_groups=mesh['frame'=4,'vox_0'=8,'vox_1'=8,'vox_2'=2] {'vox_0','vox_1','vox_2'}, dimensions={0} | all-to-all | bytes 1048576 | tf_op jit(solution)/shard_map/all_to_all | solution.py:16
  38.9 2.9 %folded_gram.1 = f32[320,128]{1,0:T(8,128)} custom-call(f32[256,4,128]{2,1,0:T(4,128)} %bitcast.7), custom_call_target="tpu_custom_call" | custom-call | tf_op jit(solution)/shard_map/folded_gram/pallas_call | solution.py:57
  41.7 11.9 %all_to_all.26 = f32[8,40,128]{2,1,0:T(8,128)S(1)} all-to-all(f32[8,40,128]{2,1,0:T(8,128)} %bitcast.10), channel_id=1, replica_groups=mesh['frame'=4,'vox_0'=8,'vox_1'=8,'vox_2'=2] {'frame','vox_2'}, dimensions={0} | all-to-all | bytes 327680 | tf_op jit(solution)/shard_map/all_to_all | solution.py:16
  53.7 10.7 %all_to_all.27 = f32[8,40,128]{2,1,0:T(8,128)S(1)} all-to-all(f32[8,40,128]{2,1,0:T(8,128)S(1)} %broadcast_in_dim.9), channel_id=1, replica_groups=mesh['frame'=4,'vox_0'=8,'vox_1'=8,'vox_2'=2] {'vox_0'}, dimensions={0} | all-to-all | bytes 327680 | tf_op jit(solution)/shard_map/all_to_all | solution.py:16
  64.4 10.8 %all_to_all.28 = f32[8,40,128]{2,1,0:T(8,128)S(1)} all-to-all(f32[8,40,128]{2,1,0:T(8,128)S(1)} %broadcast_in_dim.10), channel_id=1, replica_groups=mesh['frame'=4,'vox_0'=8,'vox_1'=8,'vox_2'=2] {'vox_1'}, dimensions={0} | all-to-all | bytes 327680 | tf_op jit(solution)/shard_map/all_to_all | solution.py:16
  75.2 12.1 %all_to_all.29 = f32[8,40,128]{2,1,0:T(8,128)} all-to-all(f32[8,40,128]{2,1,0:T(8,128)S(1)} %broadcast_in_dim.11), channel_id=1, replica_groups=mesh['frame'=4,'vox_0'=8,'vox_1'=8,'vox_2'=2] {'frame','vox_2'}, dimensions={0} | all-to-all | bytes 327680 | tf_op jit(solution)/shard_map/all_to_all | solution.py:16
  87.3 11.2 %factor.1 = f32[256,256]{1,0:T(8,128)} custom-call(f32[320,128]{1,0:T(8,128)} %bitcast.9), custom_call_target="tpu_custom_call" | custom-call | tf_op jit(solution)/shard_map/factor/pallas_call | solution.py:140
  (6 shorter events, 0.1 us)

commit v3 on v2

v3 whole, which is shorter than its diff:
```python
import jax
import jax.numpy as jnp
from jax import lax
from jax.experimental import pallas as pl
from jax.experimental.pallas import tpu as pltpu
from jax.sharding import Mesh
from jax.sharding import PartitionSpec as P

VOX = ("vox_0", "vox_1", "vox_2")
PAIR = ("frame", "vox_2")
LANES = 128
SUBS = 8
GROUP = 4

def row_of(x, k):
    return jnp.broadcast_to(x[k : k + 1, :], x.shape)

def lane_of(x, k):
    return jnp.broadcast_to(x[:, k : k + 1], (x.shape[0], LANES))

def crossed(a, b):
    return lax.dot_general(a, b, (((0,), (0,)), ((), ())), precision=lax.Precision.HIGHEST, preferred_element_type=jnp.float32)

def straight(a, b):
    return lax.dot_general(a, b, (((1,), (0,)), ((), ())), precision=lax.Precision.HIGHEST, preferred_element_type=jnp.float32)

def factor_half(work, poison, later=None, later_at={}):
    width = work.shape[1]
    slabs = [slice(s, s + LANES) for s in range(0, width, LANES)]
    panels = LANES // SUBS
    sub = lax.broadcasted_iota(jnp.int32, (SUBS, LANES), 0)

    def rows(i):
        return slice(i * SUBS, (i + 1) * SUBS)

    current = [work[rows(0), s] for s in slabs]
    for j in range(panels):
        here = [lane_of(current[0], j * SUBS + k) for k in range(SUBS)]
        more = j + 1 < panels
        join = (j + 1) % GROUP != 0
        if more and join:
            ahead = [work[rows(j + 1), s] for s in slabs]
            below = [lane_of(ahead[0], j * SUBS + k) for k in range(SUBS)]
        done = [jnp.zeros((SUBS, LANES), jnp.float32) for _ in slabs]
        lines = []
        for k in range(SUBS):
            inverse = lax.rsqrt(row_of(here[k], k))
            poison = poison + inverse * 0.0
            column = here[k] * inverse
            line = [row_of(c, k) * inverse for c in current]
            lines.append(line)
            if more and join:
                lower = below[k] * inverse
                ahead = [a - lower * y for a, y in zip(ahead, line)]
            for l in range(k + 1, SUBS):
                pick = row_of(column, l)
                here[l] = here[l] - column * pick
                if more and join:
                    below[l] = below[l] - lower * pick
            if k + 1 < SUBS:
                current = [c - column * y for c, y in zip(current, line)]
            done = [jnp.where(sub == k, y, d) for y, d in zip(line, done)]
        for s, d in zip(slabs, done):
            work[rows(j), s] = d
        near = GROUP * (j // GROUP) + GROUP
        if j + 2 < near:
            turned = done[0].T
            far = range(j + 2, near)
            value = {(i, n): work[rows(i), s] for i in far for n, s in enumerate(slabs)}
            for k in range(SUBS):
                for i in far:
                    factor = lane_of(turned[rows(i), :], k)
                    for n, y in enumerate(lines[k]):
                        value[i, n] = value[i, n] - factor * y
            for i in far:
                for n, s in enumerate(slabs):
                    work[rows(i), s] = value[i, n]
        if j + 1 == near and more:
            strip = work[(near - GROUP) * SUBS : near * SUBS, :]
            rest = slice(near * SUBS, LANES)
            turned = strip[:, 0:LANES].T
            for part in (slice(near * SUBS, (near + GROUP) * SUBS), slice((near + GROUP) * SUBS, LANES)):
                if part.start < LANES:
                    work[part, :] -= straight(turned[part, :], strip)
            ahead = [work[rows(j + 1), s] for s in slabs]
        if later is not None and j in later_at:
            strip = work[later_at[j] * SUBS : (j + 1) * SUBS, LANES:]
            later[...] -= crossed(strip, strip)
        if more:
            current = ahead
    return poison

def factor_body(half, x_ref, out_ref, first, second):
    r = lax.broadcasted_iota(jnp.int32, (half, half), 0)
    c = lax.broadcasted_iota(jnp.int32, (half, half), 1)
    folded = x_ref[0:half, :]
    turned = folded.T
    first[:, 0:half] = jnp.where(r >= c, folded, turned)
    first[:, half:] = x_ref[half : 2 * half, :]
    second[...] = jnp.where(r == c, x_ref[2 * half : 2 * half + 1, :], jnp.where(r < c, folded, turned))
    poison = factor_half(first, jnp.zeros((SUBS, LANES), jnp.float32), second, {7: 0, 13: 8, 15: 14})
    across = first[:, half:]
    out_ref[0:half, half:] = jnp.zeros((half, half), jnp.float32)
    poison = factor_half(second, poison)
    spoil = poison[0:1, :]
    out_ref[half:, 0:half] = across.T + spoil
    out_ref[0:half, 0:half] = jnp.where(r >= c, first[:, 0:half].T + spoil, 0.0)
    out_ref[half:, half:] = jnp.where(r >= c, second[...].T + spoil, 0.0)

def factor(whole, half):
    return pl.pallas_call(
        lambda *refs: factor_body(half, *refs),
        out_shape=jax.ShapeDtypeStruct((2 * half, 2 * half), jnp.float32),
        scratch_shapes=[pltpu.VMEM((half, 2 * half), jnp.float32), pltpu.VMEM((half, half), jnp.float32)],
        compiler_params=pltpu.CompilerParams(vmem_limit_bytes=8 << 20),
        name="factor",
    )(whole)

def exchange(tiles, axes):
    return lax.all_to_all(tiles, axes, split_axis=0, concat_axis=0, tiled=True)


def from_everyone(x, axes):
    return exchange(jnp.broadcast_to(x, (lax.axis_size(axes), *x.shape)), axes)


def folded_gram(columns, column_total, padded):
    half = columns.shape[0] // 2
    flat = columns.reshape(2 * half, -1)
    gram = jnp.dot(
        flat,
        flat.T,
        precision=lax.Precision.HIGHEST,
        preferred_element_type=jnp.float32,
    ) / jnp.float32(column_total)
    r = lax.broadcasted_iota(jnp.int32, (half, half), 0)
    c = lax.broadcasted_iota(jnp.int32, (half, half), 1)
    low = gram[half:, half:]
    diagonal = jnp.sum(jnp.where(r == c, low, 0.0), axis=0, keepdims=True)
    return jnp.concatenate(
        [
            jnp.where(r >= c, gram[:half, :half], low),
            gram[:half, half:],
            jnp.broadcast_to(diagonal, (padded - 2 * half, half)),
        ]
    )


def per_device(volume):
    _, rows_z, lines, width = volume.shape
    voxes = lax.axis_size(VOX)
    half = rows_z * voxes // 2
    column_total = float(lax.axis_size("frame") * lines * width)
    tiles = volume.reshape(rows_z, voxes, lines // voxes, width).swapaxes(0, 1)
    columns = exchange(tiles, VOX).reshape(2 * half, lines // voxes, width)
    pair = lax.axis_size(PAIR)
    share = -(-(2 * half + 1) // (8 * pair)) * 8
    folded = folded_gram(columns, column_total, share * pair)
    part = jnp.sum(exchange(folded.reshape(pair, share, half), PAIR), axis=0)
    part = jnp.sum(from_everyone(part, "vox_0"), axis=0)
    part = jnp.sum(from_everyone(part, "vox_1"), axis=0)
    whole = from_everyone(part, PAIR).reshape(pair * share, half)
    return factor(whole, half)


def solution(mesh):
    finer = Mesh(
        mesh.devices.reshape(mesh.shape["frame"], 8, 8, 2), ("frame", "vox_0", "vox_1", "vox_2")
    )
    return jax.shard_map(
        per_device,
        mesh=finer,
        in_specs=(P("frame", VOX, None, None),),
        out_specs=P(),
        check_vma=False,
    )
```

time: 99 us -> 94.5 us (0.955)
  Pallas kernels: 14.1 us -> 10 us
  blocking collectives: 83.2 us -> 82.2 us
    pallas_call x1 -> x0, Pallas kernels: 2.88 us -> none  [folded_gram(): pl.pallas_call(body, out_shape=jax.ShapeDtypeStruct((padded, half), jnp.f...]
    pallas_call x1, Pallas kernels: 11.2 us -> 10 us  [factor(): pl.pallas_call(lambda *refs: factor_body(half, *refs), out_shape=jax.Shap...]
where the time goes in v3:
time: 94.5 us; the launch traced here: 94.2 us
  blocking collectives  82.2 us (87%)
  Pallas kernels  10 us (11%)
  local copies, waits for them, and re-layouts  1.18 us (1%)
    all_to_all x5, blocking collectives, exchange(): return lax.all_to_all(tiles, axes, split_axis=0, concat_axis=0, tiled=True)  82.2 us
    pallas_call x1, Pallas kernels, factor(): pl.pallas_call(lambda *refs: factor_body(half, *refs), out_shape=jax.Shap...  10 us

profile of v3, /device:TPU:1, one launch (start us, length us, event | category | flops | bytes accessed | tf_op | source)
XLA Modules:
  0.0 94.2 jit_solution(15239752944149369451)
XLA Ops:
  0.0 1.1 %copy.10 = f32[2,128,4,128]{3,2,0,1:T(4,128)S(1)} copy(f32[2,128,4,128]{3,2,1,0:T(4,128)} %bitcast.15) | data formatting | bytes 1048576 | tf_op jit(solution)/shard_map/reshape | solution.py:154
  1.1 37.6 %all_to_all.25 = f32[128,2,4,128]{3,2,1,0:T(4,128)S(1)} all-to-all(f32[128,2,4,128]{3,2,1,0:T(4,128)S(1)} %bitcast.13), channel_id=1, replica_groups=mesh['frame'=4,'vox_0'=8,'vox_1'=8,'vox_2'=2] {'vox_0','vox_1','vox_2'}, dimensions={0} | all-to-all | bytes 1048576 | tf_op jit(solution)/shard_map/all_to_all | solution.py:120
  38.8 0.6 convolution_multiply_fusion
  39.5 11.7 %all_to_all.26 = f32[8,40,128]{2,1,0:T(8,128)S(1)} all-to-all(f32[8,40,128]{2,1,0:T(8,128)S(1)} %bitcast.14), channel_id=1, replica_groups=mesh['frame'=4,'vox_0'=8,'vox_1'=8,'vox_2'=2] {'frame','vox_2'}, dimensions={0} | all-to-all | bytes 327680 | tf_op jit(solution)/shard_map/all_to_all | solution.py:120
  51.2 10.7 %all_to_all.27 = f32[8,40,128]{2,1,0:T(8,128)S(1)} all-to-all(f32[8,40,128]{2,1,0:T(8,128)S(1)} %broadcast_in_dim.21), channel_id=1, replica_groups=mesh['frame'=4,'vox_0'=8,'vox_1'=8,'vox_2'=2] {'vox_0'}, dimensions={0} | all-to-all | bytes 327680 | tf_op jit(solution)/shard_map/all_to_all | solution.py:120
  61.9 10.8 %all_to_all.28 = f32[8,40,128]{2,1,0:T(8,128)S(1)} all-to-all(f32[8,40,128]{2,1,0:T(8,128)S(1)} %broadcast_in_dim.22), channel_id=1, replica_groups=mesh['frame'=4,'vox_0'=8,'vox_1'=8,'vox_2'=2] {'vox_1'}, dimensions={0} | all-to-all | bytes 327680 | tf_op jit(solution)/shard_map/all_to_all | solution.py:120
  72.7 11.4 %all_to_all.29 = f32[8,40,128]{2,1,0:T(8,128)S(1)} all-to-all(f32[8,40,128]{2,1,0:T(8,128)S(1)} %broadcast_in_dim.23), channel_id=1, replica_groups=mesh['frame'=4,'vox_0'=8,'vox_1'=8,'vox_2'=2] {'frame','vox_2'}, dimensions={0} | all-to-all | bytes 327680 | tf_op jit(solution)/shard_map/all_to_all | solution.py:120
  84.2 10.0 %factor.1 = f32[256,256]{1,0:T(8,128)} custom-call(f32[320,128]{1,0:T(8,128)S(1)} %bitcast.11), custom_call_target="tpu_custom_call" | custom-call | tf_op jit(solution)/shard_map/factor/pallas_call | solution.py:111
  (9 shorter events, 0.1 us)

commit v4 on v3

--- a/solution.py
+++ b/solution.py
@@ -10,6 +10,7 @@
 PAIR = ("frame", "vox_2")
 LANES = 128
 SUBS = 8
+TALL = 4
 GROUP = 4
 
 def row_of(x, k):
@@ -154,9 +155,9 @@
     tiles = volume.reshape(rows_z, voxes, lines // voxes, width).swapaxes(0, 1)
     columns = exchange(tiles, VOX).reshape(2 * half, lines // voxes, width)
     pair = lax.axis_size(PAIR)
-    share = -(-(2 * half + 1) // (8 * pair)) * 8
+    share = -(-(2 * half + 1) // (TALL * pair)) * TALL
     folded = folded_gram(columns, column_total, share * pair)
-    part = jnp.sum(exchange(folded.reshape(pair, share, half), PAIR), axis=0)
+    part = jnp.sum(exchange(folded.reshape(pair, share // TALL, TALL, half), PAIR), axis=0)
     part = jnp.sum(from_everyone(part, "vox_0"), axis=0)
     part = jnp.sum(from_everyone(part, "vox_1"), axis=0)
     whole = from_everyone(part, PAIR).reshape(pair * share, half)

time: 94.5 us -> 93.7 us (level)
  no operation moved by 1% of the time
where the time goes in v4:
time: 93.7 us; the launch traced here: 93.4 us
  blocking collectives  81.4 us (87%)
  Pallas kernels  10 us (11%)
  local copies, waits for them, and re-layouts  1.2 us (1%)
    all_to_all x5, blocking collectives, exchange(): return lax.all_to_all(tiles, axes, split_axis=0, concat_axis=0, tiled=True)  81.4 us
    pallas_call x1, Pallas kernels, factor(): pl.pallas_call(lambda *refs: factor_body(half, *refs), out_shape=jax.Shap...  10 us

profile of v4, /device:TPU:1, one launch (start us, length us, event | category | flops | bytes accessed | tf_op | source)
XLA Modules:
  0.0 93.4 jit_solution(7101262830070244308)
XLA Ops:
  0.0 1.1 %copy.15 = f32[2,128,4,128]{3,2,0,1:T(4,128)S(1)} copy(f32[2,128,4,128]{3,2,1,0:T(4,128)} %bitcast.15) | data formatting | bytes 1048576 | tf_op jit(solution)/shard_map/reshape | solution.py:155
  1.1 37.6 %all_to_all.25 = f32[128,2,4,128]{3,2,1,0:T(4,128)S(1)} all-to-all(f32[128,2,4,128]{3,2,1,0:T(4,128)S(1)} %bitcast.13), channel_id=1, replica_groups=mesh['frame'=4,'vox_0'=8,'vox_1'=8,'vox_2'=2] {'vox_0','vox_1','vox_2'}, dimensions={0} | all-to-all | bytes 1048576 | tf_op jit(solution)/shard_map/all_to_all | solution.py:121
  38.8 0.6 convolution_multiply_fusion
  39.5 11.6 %all_to_all.26 = f32[8,9,4,128]{3,2,1,0:T(4,128)S(1)} all-to-all(f32[8,9,4,128]{3,2,1,0:T(4,128)S(1)} %bitcast.14), channel_id=1, replica_groups=mesh['frame'=4,'vox_0'=8,'vox_1'=8,'vox_2'=2] {'frame','vox_2'}, dimensions={0} | all-to-all | bytes 294912 | tf_op jit(solution)/shard_map/all_to_all | solution.py:121
  51.1 10.3 %all_to_all.27 = f32[8,9,4,128]{3,2,1,0:T(4,128)S(1)} all-to-all(f32[8,9,4,128]{3,2,1,0:T(4,128)S(1)} %broadcast_in_dim.21), channel_id=1, replica_groups=mesh['frame'=4,'vox_0'=8,'vox_1'=8,'vox_2'=2] {'vox_0'}, dimensions={0} | all-to-all | bytes 294912 | tf_op jit(solution)/shard_map/all_to_all | solution.py:121
  61.5 10.6 %all_to_all.28 = f32[8,9,4,128]{3,2,1,0:T(4,128)S(1)} all-to-all(f32[8,9,4,128]{3,2,1,0:T(4,128)S(1)} %broadcast_in_dim.22), channel_id=1, replica_groups=mesh['frame'=4,'vox_0'=8,'vox_1'=8,'vox_2'=2] {'vox_1'}, dimensions={0} | all-to-all | bytes 294912 | tf_op jit(solution)/shard_map/all_to_all | solution.py:121
  72.1 11.3 %all_to_all.29 = f32[8,9,4,128]{3,2,1,0:T(4,128)S(1)} all-to-all(f32[8,9,4,128]{3,2,1,0:T(4,128)S(1)} %broadcast_in_dim.23), channel_id=1, replica_groups=mesh['frame'=4,'vox_0'=8,'vox_1'=8,'vox_2'=2] {'frame','vox_2'}, dimensions={0} | all-to-all | bytes 294912 | tf_op jit(solution)/shard_map/all_to_all | solution.py:121
  83.4 10.0 %factor.1 = f32[256,256]{1,0:T(8,128)} custom-call(f32[288,128]{1,0:T(8,128)S(1)} %bitcast.11), custom_call_target="tpu_custom_call" | custom-call | tf_op jit(solution)/shard_map/factor/pallas_call | solution.py:112
  (9 shorter events, 0.2 us)

commit v5 on v4

--- a/solution.py
+++ b/solution.py
@@ -29,66 +29,49 @@
     width = work.shape[1]
     slabs = [slice(s, s + LANES) for s in range(0, width, LANES)]
     panels = LANES // SUBS
+    wide = GROUP * SUBS
     sub = lax.broadcasted_iota(jnp.int32, (SUBS, LANES), 0)
 
     def rows(i):
         return slice(i * SUBS, (i + 1) * SUBS)
 
-    current = [work[rows(0), s] for s in slabs]
-    for j in range(panels):
-        here = [lane_of(current[0], j * SUBS + k) for k in range(SUBS)]
-        more = j + 1 < panels
-        join = (j + 1) % GROUP != 0
-        if more and join:
-            ahead = [work[rows(j + 1), s] for s in slabs]
-            below = [lane_of(ahead[0], j * SUBS + k) for k in range(SUBS)]
-        done = [jnp.zeros((SUBS, LANES), jnp.float32) for _ in slabs]
-        lines = []
-        for k in range(SUBS):
-            inverse = lax.rsqrt(row_of(here[k], k))
+    for first in range(0, panels, GROUP):
+        band = [[work[rows(first + i), s] for s in slabs] for i in range(GROUP)]
+        left = {}
+        for m in range(wide):
+            for i in range(m // SUBS, GROUP):
+                left[m, i] = lane_of(band[i][0], first * SUBS + m)
+        done = [[jnp.zeros((SUBS, LANES), jnp.float32) for _ in slabs] for _ in range(GROUP)]
+        pivot = row_of(left[0, 0], 0)
+        for m in range(wide):
+            b, k = divmod(m, SUBS)
+            inverse = lax.rsqrt(pivot)
             poison = poison + inverse * 0.0
-            column = here[k] * inverse
-            line = [row_of(c, k) * inverse for c in current]
-            lines.append(line)
-            if more and join:
-                lower = below[k] * inverse
-                ahead = [a - lower * y for a, y in zip(ahead, line)]
-            for l in range(k + 1, SUBS):
-                pick = row_of(column, l)
-                here[l] = here[l] - column * pick
-                if more and join:
-                    below[l] = below[l] - lower * pick
-            if k + 1 < SUBS:
-                current = [c - column * y for c, y in zip(current, line)]
-            done = [jnp.where(sub == k, y, d) for y, d in zip(line, done)]
-        for s, d in zip(slabs, done):
-            work[rows(j), s] = d
-        near = GROUP * (j // GROUP) + GROUP
-        if j + 2 < near:
-            turned = done[0].T
-            far = range(j + 2, near)
-            value = {(i, n): work[rows(i), s] for i in far for n, s in enumerate(slabs)}
-            for k in range(SUBS):
-                for i in far:
-                    factor = lane_of(turned[rows(i), :], k)
-                    for n, y in enumerate(lines[k]):
-                        value[i, n] = value[i, n] - factor * y
-            for i in far:
-                for n, s in enumerate(slabs):
-                    work[rows(i), s] = value[i, n]
-        if j + 1 == near and more:
-            strip = work[(near - GROUP) * SUBS : near * SUBS, :]
+            column = {i: left[m, i] * inverse for i in range(b, GROUP)}
+            line = [row_of(c, k) * inverse for c in band[b]]
+            if m + 1 < wide:
+                b1, k1 = divmod(m + 1, SUBS)
+                next_pick = row_of(left[m, b1], k1) * inverse
+                pivot = row_of(left[m + 1, b1], k1) - next_pick * next_pick
+            for l in range(m + 1, wide):
+                bl, kl = divmod(l, SUBS)
+                pick = next_pick if l == m + 1 else row_of(column[bl], kl)
+                for i in range(bl, GROUP):
+                    left[l, i] = left[l, i] - column[i] * pick
+            done[b] = [jnp.where(sub == k, y, d) for y, d in zip(line, done[b])]
+            for i in range(b if k + 1 < SUBS else b + 1, GROUP):
+                band[i] = [v - column[i] * y for v, y in zip(band[i], line)]
+        for i in range(GROUP):
+            for s, d in zip(slabs, done[i]):
+                work[rows(first + i), s] = d
+        near = first + GROUP
+        if near < panels:
+            strip = work[first * SUBS : near * SUBS, :]
             rest = slice(near * SUBS, LANES)
-            turned = strip[:, 0:LANES].T
-            for part in (slice(near * SUBS, (near + GROUP) * SUBS), slice((near + GROUP) * SUBS, LANES)):
-                if part.start < LANES:
-                    work[part, :] -= straight(turned[part, :], strip)
-            ahead = [work[rows(j + 1), s] for s in slabs]
-        if later is not None and j in later_at:
-            strip = work[later_at[j] * SUBS : (j + 1) * SUBS, LANES:]
+            work[rest, :] -= straight(strip[:, 0:LANES].T[rest, :], strip)
+        if later is not None and near in later_at:
+            strip = work[later_at[near] * SUBS : near * SUBS, LANES:]
             later[...] -= crossed(strip, strip)
-        if more:
-            current = ahead
     return poison
 
 def factor_body(half, x_ref, out_ref, first, second):
@@ -99,7 +82,7 @@
     first[:, 0:half] = jnp.where(r >= c, folded, turned)
     first[:, half:] = x_ref[half : 2 * half, :]
     second[...] = jnp.where(r == c, x_ref[2 * half : 2 * half + 1, :], jnp.where(r < c, folded, turned))
-    poison = factor_half(first, jnp.zeros((SUBS, LANES), jnp.float32), second, {7: 0, 13: 8, 15: 14})
+    poison = factor_half(first, jnp.zeros((SUBS, LANES), jnp.float32), second, {8: 0, 12: 8, 16: 12})
     across = first[:, half:]
     out_ref[0:half, half:] = jnp.zeros((half, half), jnp.float32)
     poison = factor_half(second, poison)
@@ -116,6 +99,7 @@
         compiler_params=pltpu.CompilerParams(vmem_limit_bytes=8 << 20),
         name="factor",
     )(whole)
+
 
 def exchange(tiles, axes):
     return lax.all_to_all(tiles, axes, split_axis=0, concat_axis=0, tiled=True)

time: 93.7 us -> 90.9 us (0.970)
  Pallas kernels: 10 us -> 7.2 us
    pallas_call x1, Pallas kernels: 10 us -> 7.2 us  [factor(): pl.pallas_call(lambda *refs: factor_body(half, *refs), out_shape=jax.Shap...]
where the time goes in v5:
time: 90.9 us; the launch traced here: 90.6 us
  blocking collectives  81.4 us (90%)
  Pallas kernels  7.2 us (8%)
  local copies, waits for them, and re-layouts  1.2 us (1%)
    all_to_all x5, blocking collectives, exchange(): return lax.all_to_all(tiles, axes, split_axis=0, concat_axis=0, tiled=True)  81.4 us
    pallas_call x1, Pallas kernels, factor(): pl.pallas_call(lambda *refs: factor_body(half, *refs), out_shape=jax.Shap...  7.2 us

profile of v5, /device:TPU:1, one launch (start us, length us, event | category | flops | bytes accessed | tf_op | source)
XLA Modules:
  0.0 90.6 jit_solution(11763558156983457895)
XLA Ops:
  0.0 1.1 %copy.15 = f32[2,128,4,128]{3,2,0,1:T(4,128)S(1)} copy(f32[2,128,4,128]{3,2,1,0:T(4,128)} %bitcast.15) | data formatting | bytes 1048576 | tf_op jit(solution)/shard_map/reshape | solution.py:139
  1.1 37.6 %all_to_all.25 = f32[128,2,4,128]{3,2,1,0:T(4,128)S(1)} all-to-all(f32[128,2,4,128]{3,2,1,0:T(4,128)S(1)} %bitcast.13), channel_id=1, replica_groups=mesh['frame'=4,'vox_0'=8,'vox_1'=8,'vox_2'=2] {'vox_0','vox_1','vox_2'}, dimensions={0} | all-to-all | bytes 1048576 | tf_op jit(solution)/shard_map/all_to_all | solution.py:105
  38.8 0.6 convolution_multiply_fusion
  39.5 11.6 %all_to_all.26 = f32[8,9,4,128]{3,2,1,0:T(4,128)S(1)} all-to-all(f32[8,9,4,128]{3,2,1,0:T(4,128)S(1)} %bitcast.14), channel_id=1, replica_groups=mesh['frame'=4,'vox_0'=8,'vox_1'=8,'vox_2'=2] {'frame','vox_2'}, dimensions={0} | all-to-all | bytes 294912 | tf_op jit(solution)/shard_map/all_to_all | solution.py:105
  51.1 10.3 %all_to_all.27 = f32[8,9,4,128]{3,2,1,0:T(4,128)S(1)} all-to-all(f32[8,9,4,128]{3,2,1,0:T(4,128)S(1)} %broadcast_in_dim.21), channel_id=1, replica_groups=mesh['frame'=4,'vox_0'=8,'vox_1'=8,'vox_2'=2] {'vox_0'}, dimensions={0} | all-to-all | bytes 294912 | tf_op jit(solution)/shard_map/all_to_all | solution.py:105
  61.5 10.6 %all_to_all.28 = f32[8,9,4,128]{3,2,1,0:T(4,128)S(1)} all-to-all(f32[8,9,4,128]{3,2,1,0:T(4,128)S(1)} %broadcast_in_dim.22), channel_id=1, replica_groups=mesh['frame'=4,'vox_0'=8,'vox_1'=8,'vox_2'=2] {'vox_1'}, dimensions={0} | all-to-all | bytes 294912 | tf_op jit(solution)/shard_map/all_to_all | solution.py:105
  72.1 11.3 %all_to_all.29 = f32[8,9,4,128]{3,2,1,0:T(4,128)S(1)} all-to-all(f32[8,9,4,128]{3,2,1,0:T(4,128)S(1)} %broadcast_in_dim.23), channel_id=1, replica_groups=mesh['frame'=4,'vox_0'=8,'vox_1'=8,'vox_2'=2] {'frame','vox_2'}, dimensions={0} | all-to-all | bytes 294912 | tf_op jit(solution)/shard_map/all_to_all | solution.py:105
  83.4 7.2 %factor.1 = f32[256,256]{1,0:T(8,128)} custom-call(f32[288,128]{1,0:T(8,128)S(1)} %bitcast.11), custom_call_target="tpu_custom_call" | custom-call | tf_op jit(solution)/shard_map/factor/pallas_call | solution.py:95
  (9 shorter events, 0.2 us)

commit v6 on v5

--- a/solution.py
+++ b/solution.py
@@ -12,6 +12,7 @@
 SUBS = 8
 TALL = 4
 GROUP = 4
+SPAN = 16
 
 def row_of(x, k):
     return jnp.broadcast_to(x[k : k + 1, :], x.shape)
@@ -19,11 +20,27 @@
 def lane_of(x, k):
     return jnp.broadcast_to(x[:, k : k + 1], (x.shape[0], LANES))
 
-def crossed(a, b):
-    return lax.dot_general(a, b, (((0,), (0,)), ((), ())), precision=lax.Precision.HIGHEST, preferred_element_type=jnp.float32)
+def pieces(x):
+    high = x.astype(jnp.bfloat16)
+    rest = x - high.astype(jnp.float32)
+    middle = rest.astype(jnp.bfloat16)
+    low = (rest - middle.astype(jnp.float32)).astype(jnp.bfloat16)
+    return high, middle, low
 
-def straight(a, b):
-    return lax.dot_general(a, b, (((1,), (0,)), ((), ())), precision=lax.Precision.HIGHEST, preferred_element_type=jnp.float32)
+
+def crossed(tall, flat, start=0):
+    high, middle, low = (p.astype(jnp.float32) for p in pieces(tall))
+    turned = jnp.concatenate([high, middle, low, high]).T.astype(jnp.bfloat16)
+    high, middle, low = pieces(flat)
+    none = jnp.zeros_like(high)
+    turned = turned[start:]
+    return lax.dot_general(
+        jnp.concatenate([turned, turned], axis=1),
+        jnp.concatenate([high, high, high, low, middle, middle, none, none]),
+        (((1,), (0,)), ((), ())),
+        preferred_element_type=jnp.float32,
+    )
+
 
 def factor_half(work, poison, later=None, later_at={}):
     width = work.shape[1]
@@ -37,23 +54,25 @@
 
     for first in range(0, panels, GROUP):
         band = [[work[rows(first + i), s] for s in slabs] for i in range(GROUP)]
+        done = [[jnp.zeros((SUBS, LANES), jnp.float32) for _ in slabs] for _ in range(GROUP)]
         left = {}
         for m in range(wide):
-            for i in range(m // SUBS, GROUP):
-                left[m, i] = lane_of(band[i][0], first * SUBS + m)
-        done = [[jnp.zeros((SUBS, LANES), jnp.float32) for _ in slabs] for _ in range(GROUP)]
-        pivot = row_of(left[0, 0], 0)
-        for m in range(wide):
             b, k = divmod(m, SUBS)
+            end = m - m % SPAN + SPAN
+            if m % SPAN == 0:
+                for n in range(m, end):
+                    for i in range(n // SUBS, GROUP):
+                        left[n, i] = lane_of(band[i][0], first * SUBS + n)
+                pivot = row_of(left[m, b], k)
             inverse = lax.rsqrt(pivot)
             poison = poison + inverse * 0.0
             column = {i: left[m, i] * inverse for i in range(b, GROUP)}
             line = [row_of(c, k) * inverse for c in band[b]]
-            if m + 1 < wide:
+            if m + 1 < end:
                 b1, k1 = divmod(m + 1, SUBS)
                 next_pick = row_of(left[m, b1], k1) * inverse
                 pivot = row_of(left[m + 1, b1], k1) - next_pick * next_pick
-            for l in range(m + 1, wide):
+            for l in range(m + 1, end):
                 bl, kl = divmod(l, SUBS)
                 pick = next_pick if l == m + 1 else row_of(column[bl], kl)
                 for i in range(bl, GROUP):
@@ -68,7 +87,7 @@
         if near < panels:
             strip = work[first * SUBS : near * SUBS, :]
             rest = slice(near * SUBS, LANES)
-            work[rest, :] -= straight(strip[:, 0:LANES].T[rest, :], strip)
+            work[rest, :] -= crossed(strip[:, 0:LANES], strip, near * SUBS)
         if later is not None and near in later_at:
             strip = work[later_at[near] * SUBS : near * SUBS, LANES:]
             later[...] -= crossed(strip, strip)
@@ -82,7 +101,7 @@
     first[:, 0:half] = jnp.where(r >= c, folded, turned)
     first[:, half:] = x_ref[half : 2 * half, :]
     second[...] = jnp.where(r == c, x_ref[2 * half : 2 * half + 1, :], jnp.where(r < c, folded, turned))
-    poison = factor_half(first, jnp.zeros((SUBS, LANES), jnp.float32), second, {8: 0, 12: 8, 16: 12})
+    poison = factor_half(first, jnp.zeros((SUBS, LANES), jnp.float32), second, {4: 0, 8: 4, 12: 8, 16: 12})
     across = first[:, half:]
     out_ref[0:half, half:] = jnp.zeros((half, half), jnp.float32)
     poison = factor_half(second, poison)

time: 90.9 us -> 90.4 us (level)
  no operation moved by 1% of the time
where the time goes in v6:
time: 90.4 us; the launch traced here: 90.1 us
  blocking collectives  81.4 us (90%)
  Pallas kernels  6.69 us (7%)
  local copies, waits for them, and re-layouts  1.2 us (1%)
    all_to_all x5, blocking collectives, exchange(): return lax.all_to_all(tiles, axes, split_axis=0, concat_axis=0, tiled=True)  81.4 us
    pallas_call x1, Pallas kernels, factor(): pl.pallas_call(lambda *refs: factor_body(half, *refs), out_shape=jax.Shap...  6.69 us

profile of v6, /device:TPU:1, one launch (start us, length us, event | category | flops | bytes accessed | tf_op | source)
XLA Modules:
  0.0 90.1 jit_solution(9960920174199918981)
XLA Ops:
  0.0 1.1 %copy.15 = f32[2,128,4,128]{3,2,0,1:T(4,128)S(1)} copy(f32[2,128,4,128]{3,2,1,0:T(4,128)} %bitcast.15) | data formatting | bytes 1048576 | tf_op jit(solution)/shard_map/reshape | solution.py:158
  1.1 37.6 %all_to_all.25 = f32[128,2,4,128]{3,2,1,0:T(4,128)S(1)} all-to-all(f32[128,2,4,128]{3,2,1,0:T(4,128)S(1)} %bitcast.13), channel_id=1, replica_groups=mesh['frame'=4,'vox_0'=8,'vox_1'=8,'vox_2'=2] {'vox_0','vox_1','vox_2'}, dimensions={0} | all-to-all | bytes 1048576 | tf_op jit(solution)/shard_map/all_to_all | solution.py:124
  38.8 0.6 convolution_multiply_fusion
  39.5 11.6 %all_to_all.26 = f32[8,9,4,128]{3,2,1,0:T(4,128)S(1)} all-to-all(f32[8,9,4,128]{3,2,1,0:T(4,128)S(1)} %bitcast.14), channel_id=1, replica_groups=mesh['frame'=4,'vox_0'=8,'vox_1'=8,'vox_2'=2] {'frame','vox_2'}, dimensions={0} | all-to-all | bytes 294912 | tf_op jit(solution)/shard_map/all_to_all | solution.py:124
  51.1 10.3 %all_to_all.27 = f32[8,9,4,128]{3,2,1,0:T(4,128)S(1)} all-to-all(f32[8,9,4,128]{3,2,1,0:T(4,128)S(1)} %broadcast_in_dim.21), channel_id=1, replica_groups=mesh['frame'=4,'vox_0'=8,'vox_1'=8,'vox_2'=2] {'vox_0'}, dimensions={0} | all-to-all | bytes 294912 | tf_op jit(solution)/shard_map/all_to_all | solution.py:124
  61.5 10.6 %all_to_all.28 = f32[8,9,4,128]{3,2,1,0:T(4,128)S(1)} all-to-all(f32[8,9,4,128]{3,2,1,0:T(4,128)S(1)} %broadcast_in_dim.22), channel_id=1, replica_groups=mesh['frame'=4,'vox_0'=8,'vox_1'=8,'vox_2'=2] {'vox_1'}, dimensions={0} | all-to-all | bytes 294912 | tf_op jit(solution)/shard_map/all_to_all | solution.py:124
  72.1 11.3 %all_to_all.29 = f32[8,9,4,128]{3,2,1,0:T(4,128)S(1)} all-to-all(f32[8,9,4,128]{3,2,1,0:T(4,128)S(1)} %broadcast_in_dim.23), channel_id=1, replica_groups=mesh['frame'=4,'vox_0'=8,'vox_1'=8,'vox_2'=2] {'frame','vox_2'}, dimensions={0} | all-to-all | bytes 294912 | tf_op jit(solution)/shard_map/all_to_all | solution.py:124
  83.4 6.7 %factor.1 = f32[256,256]{1,0:T(8,128)} custom-call(f32[288,128]{1,0:T(8,128)S(1)} %bitcast.11), custom_call_target="tpu_custom_call" | custom-call | tf_op jit(solution)/shard_map/factor/pallas_call | solution.py:114
  (9 shorter events, 0.2 us)

commit v7 on v6

--- a/solution.py
+++ b/solution.py
@@ -6,11 +6,11 @@
 from jax.sharding import Mesh
 from jax.sharding import PartitionSpec as P
 
-VOX = ("vox_0", "vox_1", "vox_2")
-PAIR = ("frame", "vox_2")
+VOX = ("y_far", "y_near", "z_far", "z_near", "core")
+NEAR = ("frame", "y_near", "z_near", "core")
+FAR = ("y_far", "z_far")
 LANES = 128
 SUBS = 8
-TALL = 4
 GROUP = 4
 SPAN = 16
 
@@ -124,8 +124,28 @@
     return lax.all_to_all(tiles, axes, split_axis=0, concat_axis=0, tiled=True)
 
 
-def from_everyone(x, axes):
-    return exchange(jnp.broadcast_to(x, (lax.axis_size(axes), *x.shape)), axes)
+def summed_for(tiles, count, to):
+    share = tiles.shape[0] // count
+
+    def body(tiles_ref, out_ref):
+        sums = [tiles_ref[i * share : (i + 1) * share, :] for i in range(4)]
+        for i in range(4, count):
+            sums[i % 4] = sums[i % 4] + tiles_ref[i * share : (i + 1) * share, :]
+        total = (sums[0] + sums[1]) + (sums[2] + sums[3])
+        for i in range(to):
+            out_ref[i * share : (i + 1) * share, :] = total
+
+    return pl.pallas_call(
+        body,
+        out_shape=jax.ShapeDtypeStruct((share * to, tiles.shape[1]), tiles.dtype),
+        compiler_params=pltpu.CompilerParams(vmem_limit_bytes=4 << 20),
+        name="summed_for",
+    )(tiles)
+
+
+def exchange_rows(rows, axes):
+    count = lax.axis_size(axes)
+    return exchange(rows.reshape(count, -1, 1, rows.shape[-1]), axes).reshape(rows.shape)
 
 
 def folded_gram(columns, column_total, padded):
@@ -157,19 +177,18 @@
     column_total = float(lax.axis_size("frame") * lines * width)
     tiles = volume.reshape(rows_z, voxes, lines // voxes, width).swapaxes(0, 1)
     columns = exchange(tiles, VOX).reshape(2 * half, lines // voxes, width)
-    pair = lax.axis_size(PAIR)
-    share = -(-(2 * half + 1) // (TALL * pair)) * TALL
-    folded = folded_gram(columns, column_total, share * pair)
-    part = jnp.sum(exchange(folded.reshape(pair, share // TALL, TALL, half), PAIR), axis=0)
-    part = jnp.sum(from_everyone(part, "vox_0"), axis=0)
-    part = jnp.sum(from_everyone(part, "vox_1"), axis=0)
-    whole = from_everyone(part, PAIR).reshape(pair * share, half)
+    near, far = lax.axis_size(NEAR), lax.axis_size(FAR)
+    share = -(-(2 * half + 1) // near)
+    folded = folded_gram(columns, column_total, share * near)
+    part = summed_for(exchange_rows(folded, NEAR), near, far)
+    part = summed_for(exchange_rows(part, FAR), far, near)
+    whole = exchange_rows(part, NEAR)
     return factor(whole, half)
 
 
 def solution(mesh):
     finer = Mesh(
-        mesh.devices.reshape(mesh.shape["frame"], 8, 8, 2), ("frame", "vox_0", "vox_1", "vox_2")
+        mesh.devices.reshape(mesh.shape["frame"], 4, 2, 4, 2, 2), ("frame", *VOX)
     )
     return jax.shard_map(
         per_device,

time: 90.4 us -> 87.5 us (0.968)
  blocking collectives: 81.4 us -> 78.7 us
    all_to_all x5 -> x4, blocking collectives: 81.4 us -> 78.7 us  [exchange(): return lax.all_to_all(tiles, axes, split_axis=0, concat_axis=0, tiled=True)]
where the time goes in v7:
time: 87.5 us; the launch traced here: 87.2 us
  blocking collectives  78.7 us (90%)
  Pallas kernels  6.74 us (8%)
  local copies, waits for them, and re-layouts  1.14 us (1%)
    all_to_all x4, blocking collectives, exchange(): return lax.all_to_all(tiles, axes, split_axis=0, concat_axis=0, tiled=True)  78.7 us
    pallas_call x1, Pallas kernels, factor(): pl.pallas_call(lambda *refs: factor_body(half, *refs), out_shape=jax.Shap...  6.69 us

profile of v7, /device:TPU:1, one launch (start us, length us, event | category | flops | bytes accessed | tf_op | source)
XLA Modules:
  0.0 87.2 jit_solution(14781657597083074444)
XLA Ops:
  0.0 1.1 %copy.13 = f32[2,128,4,128]{3,2,0,1:T(4,128)S(1)} copy(f32[2,128,4,128]{3,2,1,0:T(4,128)} %bitcast.23) | data formatting | bytes 1048576 | tf_op jit(solution)/shard_map/reshape | solution.py:178
  1.1 37.6 %all_to_all.20 = f32[128,2,4,128]{3,2,1,0:T(4,128)S(1)} all-to-all(f32[128,2,4,128]{3,2,1,0:T(4,128)S(1)} %bitcast.21), channel_id=1, replica_groups=mesh['frame'=4,'y_far'=4,'y_near'=2,'z_far'=4,'z_near'=2,'core'=2] {'y_f..., dimensions={0} | all-to-all | bytes 1048576 | tf_op jit(solution)/shard_map/all_to_all | solution.py:124
  38.8 0.6 convolution_multiply_fusion
  39.5 13.9 %all_to_all.21 = f32[32,9,1,128]{3,2,1,0:T(1,128)S(1)} all-to-all(f32[32,9,1,128]{3,2,1,0:T(1,128)S(1)} %bitcast.22), channel_id=1, replica_groups=mesh['frame'=4,'y_far'=4,'y_near'=2,'z_far'=4,'z_near'=2,'core'=2] {'fra..., dimensions={0} | all-to-all | bytes 294912 | tf_op jit(solution)/shard_map/all_to_all | solution.py:124
  53.4 15.2 %all_to_all.22 = f32[16,9,1,128]{3,2,1,0:T(1,128)S(1)} all-to-all(f32[16,9,1,128]{3,2,1,0:T(1,128)S(1)} %bitcast.18), channel_id=1, replica_groups=mesh['frame'=4,'y_far'=4,'y_near'=2,'z_far'=4,'z_near'=2,'core'=2] {'y_f..., dimensions={0} | all-to-all | bytes 147456 | tf_op jit(solution)/shard_map/all_to_all | solution.py:124
  68.6 11.9 %all_to_all.23 = f32[32,9,1,128]{3,2,1,0:T(1,128)S(1)} all-to-all(f32[32,9,1,128]{3,2,1,0:T(1,128)S(1)} %bitcast.17), channel_id=1, replica_groups=mesh['frame'=4,'y_far'=4,'y_near'=2,'z_far'=4,'z_near'=2,'core'=2] {'fra..., dimensions={0} | all-to-all | bytes 294912 | tf_op jit(solution)/shard_map/all_to_all | solution.py:124
  80.5 6.7 %factor.1 = f32[256,256]{1,0:T(8,128)} custom-call(f32[288,128]{1,0:T(8,128)S(1)} %bitcast.15), custom_call_target="tpu_custom_call" | custom-call | tf_op jit(solution)/shard_map/factor/pallas_call | solution.py:114
  (5 shorter events, 0.1 us)

commit v8 on v7

--- a/solution.py
+++ b/solution.py
@@ -170,13 +170,38 @@
     )
 
 
+def by_receiver(volume, voxes):
+    _, rows_z, lines, width = volume.shape
+    tiles = volume.reshape(rows_z, voxes, lines // voxes, width)
+
+    def body(*refs):
+        from_refs, to_ref, sems = refs[:rows_z], refs[rows_z], refs[rows_z + 1]
+        copies = [
+            pltpu.make_async_copy(from_ref, to_ref.at[:, z], sems.at[z])
+            for z, from_ref in enumerate(from_refs)
+        ]
+        for copy in copies:
+            copy.start()
+        for copy in copies:
+            copy.wait()
+
+    return pl.pallas_call(
+        body,
+        out_shape=jax.ShapeDtypeStruct((voxes, rows_z, lines // voxes, width), volume.dtype),
+        in_specs=[pl.BlockSpec(memory_space=pl.ANY)] * rows_z,
+        out_specs=pl.BlockSpec(memory_space=pltpu.VMEM),
+        scratch_shapes=[pltpu.SemaphoreType.DMA((rows_z,))],
+        compiler_params=pltpu.CompilerParams(vmem_limit_bytes=4 << 20),
+        name="by_receiver",
+    )(*(tiles[z] for z in range(rows_z)))
+
+
 def per_device(volume):
     _, rows_z, lines, width = volume.shape
     voxes = lax.axis_size(VOX)
     half = rows_z * voxes // 2
     column_total = float(lax.axis_size("frame") * lines * width)
-    tiles = volume.reshape(rows_z, voxes, lines // voxes, width).swapaxes(0, 1)
-    columns = exchange(tiles, VOX).reshape(2 * half, lines // voxes, width)
+    columns = exchange(by_receiver(volume, voxes), VOX).reshape(2 * half, lines // voxes, width)
     near, far = lax.axis_size(NEAR), lax.axis_size(FAR)
     share = -(-(2 * half + 1) // near)
     folded = folded_gram(columns, column_total, share * near)

time: 87.5 us -> 87.5 us (level)
    reshape x1 -> x0, local copies, waits for them, and re-layouts: 1.13 us -> none  [per_device(): tiles = volume.reshape(rows_z, voxes, lines // voxes, width).swapaxes(0, 1)]
    slice x0 -> x1, local copies, waits for them, and re-layouts: none -> 1.06 us  [by_receiver(): tiles[z]]
where the time goes in v8:
time: 87.5 us; the launch traced here: 87.3 us
  blocking collectives  78.7 us (90%)
  Pallas kernels  6.85 us (8%)
  local copies, waits for them, and re-layouts  1.07 us (1%)
    all_to_all x4, blocking collectives, exchange(): return lax.all_to_all(tiles, axes, split_axis=0, concat_axis=0, tiled=True)  78.7 us
    pallas_call x1, Pallas kernels, factor(): pl.pallas_call(lambda *refs: factor_body(half, *refs), out_shape=jax.Shap...  6.69 us

profile of v8, /device:TPU:1, one launch (start us, length us, event | category | flops | bytes accessed | tf_op | source)
XLA Modules:
  0.0 87.3 jit_solution(6296359544736578711)
XLA Ops:
  0.0 1.1 %fusion.2 = (f32[1,1,512,128]{3,2,1,0:T(8,128)S(1)}, f32[1,1,512,128]{3,2,1,0:T(8,128)S(1)}) fusion(f32[1,2,512,128]{3,2,1,0:T(8,128)} %param.1), kind=kLoop, calls=%fused_computation.8 | loop fusion | bytes 1048576 | tf_op jit(solution)/shard_map/slice | solution.py:196
  1.1 0.1 by_receiver.1
  1.2 37.6 %all_to_all.20 = f32[128,2,4,128]{3,2,1,0:T(4,128)S(1)} all-to-all(f32[128,2,4,128]{3,2,1,0:T(4,128)S(1)} %by_receiver.1), channel_id=1, replica_groups=mesh['frame'=4,'y_far'=4,'y_near'=2,'z_far'=4,'z_near'=2,'core'=2] {'y_f..., dimensions={0} | all-to-all | bytes 1048576 | tf_op jit(solution)/shard_map/all_to_all | solution.py:124
  38.8 0.6 convolution_multiply_fusion
  39.5 13.9 %all_to_all.21 = f32[32,9,1,128]{3,2,1,0:T(1,128)S(1)} all-to-all(f32[32,9,1,128]{3,2,1,0:T(1,128)S(1)} %bitcast.21), channel_id=1, replica_groups=mesh['frame'=4,'y_far'=4,'y_near'=2,'z_far'=4,'z_near'=2,'core'=2] {'fra..., dimensions={0} | all-to-all | bytes 294912 | tf_op jit(solution)/shard_map/all_to_all | solution.py:124
  53.5 15.2 %all_to_all.22 = f32[16,9,1,128]{3,2,1,0:T(1,128)S(1)} all-to-all(f32[16,9,1,128]{3,2,1,0:T(1,128)S(1)} %bitcast.18), channel_id=1, replica_groups=mesh['frame'=4,'y_far'=4,'y_near'=2,'z_far'=4,'z_near'=2,'core'=2] {'y_f..., dimensions={0} | all-to-all | bytes 147456 | tf_op jit(solution)/shard_map/all_to_all | solution.py:124
  68.7 11.9 %all_to_all.23 = f32[32,9,1,128]{3,2,1,0:T(1,128)S(1)} all-to-all(f32[32,9,1,128]{3,2,1,0:T(1,128)S(1)} %bitcast.17), channel_id=1, replica_groups=mesh['frame'=4,'y_far'=4,'y_near'=2,'z_far'=4,'z_near'=2,'core'=2] {'fra..., dimensions={0} | all-to-all | bytes 294912 | tf_op jit(solution)/shard_map/all_to_all | solution.py:124
  80.6 6.7 %factor.1 = f32[256,256]{1,0:T(8,128)} custom-call(f32[288,128]{1,0:T(8,128)S(1)} %bitcast.15), custom_call_target="tpu_custom_call" | custom-call | tf_op jit(solution)/shard_map/factor/pallas_call | solution.py:114
  (5 shorter events, 0.1 us)

commit v9 on v8

--- a/solution.py
+++ b/solution.py
@@ -93,7 +93,7 @@
             later[...] -= crossed(strip, strip)
     return poison
 
-def factor_body(half, x_ref, out_ref, first, second):
+def factor_body(half, x_ref, out_ref, first, second, full, sems):
     r = lax.broadcasted_iota(jnp.int32, (half, half), 0)
     c = lax.broadcasted_iota(jnp.int32, (half, half), 1)
     folded = x_ref[0:half, :]
@@ -102,19 +102,51 @@
     first[:, half:] = x_ref[half : 2 * half, :]
     second[...] = jnp.where(r == c, x_ref[2 * half : 2 * half + 1, :], jnp.where(r < c, folded, turned))
     poison = factor_half(first, jnp.zeros((SUBS, LANES), jnp.float32), second, {4: 0, 8: 4, 12: 8, 16: 12})
-    across = first[:, half:]
-    out_ref[0:half, half:] = jnp.zeros((half, half), jnp.float32)
+    top, left, corner = (
+        pltpu.make_async_copy(full.at[rows, cols], out_ref.at[rows, cols], sems.at[i])
+        for i, (rows, cols) in enumerate(
+            (
+                (slice(0, half), slice(0, 2 * half)),
+                (slice(half, 2 * half), slice(0, half)),
+                (slice(half, 2 * half), slice(half, 2 * half)),
+            )
+        )
+    )
+    full[0:half, half:] = jnp.zeros((half, half), jnp.float32)
+    full[0:half, 0:half] = jnp.where(r >= c, first[:, 0:half].T, 0.0)
+    top.start()
+    full[half:, 0:half] = first[:, half:].T
+    left.start()
     poison = factor_half(second, poison)
-    spoil = poison[0:1, :]
-    out_ref[half:, 0:half] = across.T + spoil
-    out_ref[0:half, 0:half] = jnp.where(r >= c, first[:, 0:half].T + spoil, 0.0)
-    out_ref[half:, half:] = jnp.where(r >= c, second[...].T + spoil, 0.0)
+    full[half:, half:] = jnp.where(r >= c, second[...].T, 0.0)
+    corner.start()
+    top.wait()
+    left.wait()
+    corner.wait()
+
+    @pl.when(jnp.logical_not(poison[0, 0] == 0.0))
+    def _():
+        spoil = poison[0:1, :]
+        full[0:half, 0:half] = jnp.where(r >= c, spoil, 0.0)
+        full[half:, 0:half] = jnp.broadcast_to(spoil, (half, half))
+        full[half:, half:] = jnp.where(r >= c, spoil, 0.0)
+        for copy in (top, left, corner):
+            copy.start()
+        for copy in (top, left, corner):
+            copy.wait()
+
 
 def factor(whole, half):
     return pl.pallas_call(
         lambda *refs: factor_body(half, *refs),
         out_shape=jax.ShapeDtypeStruct((2 * half, 2 * half), jnp.float32),
-        scratch_shapes=[pltpu.VMEM((half, 2 * half), jnp.float32), pltpu.VMEM((half, half), jnp.float32)],
+        out_specs=pl.BlockSpec(memory_space=pl.ANY),
+        scratch_shapes=[
+            pltpu.VMEM((half, 2 * half), jnp.float32),
+            pltpu.VMEM((half, half), jnp.float32),
+            pltpu.VMEM((2 * half, 2 * half), jnp.float32),
+            pltpu.SemaphoreType.DMA((3,)),
+        ],
         compiler_params=pltpu.CompilerParams(vmem_limit_bytes=8 << 20),
         name="factor",
     )(whole)

time: 87.5 us -> 87.5 us (level)
  no operation moved by 1% of the time
where the time goes in v9:
time: 87.5 us; the launch traced here: 87.2 us
  blocking collectives  78.7 us (90%)
  Pallas kernels  6.81 us (8%)
  local copies, waits for them, and re-layouts  1.07 us (1%)
    all_to_all x4, blocking collectives, exchange(): return lax.all_to_all(tiles, axes, split_axis=0, concat_axis=0, tiled=True)  78.7 us
    pallas_call x1, Pallas kernels, factor(): pl.pallas_call(lambda *refs: factor_body(half, *refs), out_shape=jax.Shap...  6.65 us

profile of v9, /device:TPU:1, one launch (start us, length us, event | category | flops | bytes accessed | tf_op | source)
XLA Modules:
  0.0 87.2 jit_solution(14745107863213148360)
XLA Ops:
  0.0 1.1 %fusion.2 = (f32[1,1,512,128]{3,2,1,0:T(8,128)S(1)}, f32[1,1,512,128]{3,2,1,0:T(8,128)S(1)}) fusion(f32[1,2,512,128]{3,2,1,0:T(8,128)} %param.1), kind=kLoop, calls=%fused_computation.8 | loop fusion | bytes 1048576 | tf_op jit(solution)/shard_map/slice | solution.py:228
  1.1 0.1 by_receiver.1
  1.2 37.6 %all_to_all.20 = f32[128,2,4,128]{3,2,1,0:T(4,128)S(1)} all-to-all(f32[128,2,4,128]{3,2,1,0:T(4,128)S(1)} %by_receiver.1), channel_id=1, replica_groups=mesh['frame'=4,'y_far'=4,'y_near'=2,'z_far'=4,'z_near'=2,'core'=2] {'y_f..., dimensions={0} | all-to-all | bytes 1048576 | tf_op jit(solution)/shard_map/all_to_all | solution.py:156
  38.8 0.6 convolution_multiply_fusion
  39.5 13.9 %all_to_all.21 = f32[32,9,1,128]{3,2,1,0:T(1,128)S(1)} all-to-all(f32[32,9,1,128]{3,2,1,0:T(1,128)S(1)} %bitcast.21), channel_id=1, replica_groups=mesh['frame'=4,'y_far'=4,'y_near'=2,'z_far'=4,'z_near'=2,'core'=2] {'fra..., dimensions={0} | all-to-all | bytes 294912 | tf_op jit(solution)/shard_map/all_to_all | solution.py:156
  53.5 15.2 %all_to_all.22 = f32[16,9,1,128]{3,2,1,0:T(1,128)S(1)} all-to-all(f32[16,9,1,128]{3,2,1,0:T(1,128)S(1)} %bitcast.18), channel_id=1, replica_groups=mesh['frame'=4,'y_far'=4,'y_near'=2,'z_far'=4,'z_near'=2,'core'=2] {'y_f..., dimensions={0} | all-to-all | bytes 147456 | tf_op jit(solution)/shard_map/all_to_all | solution.py:156
  68.7 11.9 %all_to_all.23 = f32[32,9,1,128]{3,2,1,0:T(1,128)S(1)} all-to-all(f32[32,9,1,128]{3,2,1,0:T(1,128)S(1)} %bitcast.17), channel_id=1, replica_groups=mesh['frame'=4,'y_far'=4,'y_near'=2,'z_far'=4,'z_near'=2,'core'=2] {'fra..., dimensions={0} | all-to-all | bytes 294912 | tf_op jit(solution)/shard_map/all_to_all | solution.py:156
  80.6 6.6 %factor.1 = f32[256,256]{1,0:T(8,128)} custom-call(f32[288,128]{1,0:T(8,128)S(1)} %bitcast.15), custom_call_target="tpu_custom_call" | custom-call | tf_op jit(solution)/shard_map/factor/pallas_call | solution.py:140
  (5 shorter events, 0.1 us)

commit v10 on v8

--- a/solution.py
+++ b/solution.py
@@ -65,7 +65,6 @@
                         left[n, i] = lane_of(band[i][0], first * SUBS + n)
                 pivot = row_of(left[m, b], k)
             inverse = lax.rsqrt(pivot)
-            poison = poison + inverse * 0.0
             column = {i: left[m, i] * inverse for i in range(b, GROUP)}
             line = [row_of(c, k) * inverse for c in band[b]]
             if m + 1 < end:
@@ -91,7 +90,7 @@
         if later is not None and near in later_at:
             strip = work[later_at[near] * SUBS : near * SUBS, LANES:]
             later[...] -= crossed(strip, strip)
-    return poison
+    return poison + inverse * 0.0
 
 def factor_body(half, x_ref, out_ref, first, second):
     r = lax.broadcasted_iota(jnp.int32, (half, half), 0)

time: 87.5 us -> 87.5 us (level)
  no operation moved by 1% of the time
where the time goes in v10:
time: 87.5 us; the launch traced here: 87.3 us
  blocking collectives  78.7 us (90%)
  Pallas kernels  6.84 us (8%)
  local copies, waits for them, and re-layouts  1.07 us (1%)
    all_to_all x4, blocking collectives, exchange(): return lax.all_to_all(tiles, axes, split_axis=0, concat_axis=0, tiled=True)  78.7 us
    pallas_call x1, Pallas kernels, factor(): pl.pallas_call(lambda *refs: factor_body(half, *refs), out_shape=jax.Shap...  6.68 us

profile of v10, /device:TPU:1, one launch (start us, length us, event | category | flops | bytes accessed | tf_op | source)
XLA Modules:
  0.0 87.3 jit_solution(3373419055140072598)
XLA Ops:
  0.0 1.1 %fusion.2 = (f32[1,1,512,128]{3,2,1,0:T(8,128)S(1)}, f32[1,1,512,128]{3,2,1,0:T(8,128)S(1)}) fusion(f32[1,2,512,128]{3,2,1,0:T(8,128)} %param.1), kind=kLoop, calls=%fused_computation.8 | loop fusion | bytes 1048576 | tf_op jit(solution)/shard_map/slice | solution.py:195
  1.1 0.1 by_receiver.1
  1.2 37.6 %all_to_all.20 = f32[128,2,4,128]{3,2,1,0:T(4,128)S(1)} all-to-all(f32[128,2,4,128]{3,2,1,0:T(4,128)S(1)} %by_receiver.1), channel_id=1, replica_groups=mesh['frame'=4,'y_far'=4,'y_near'=2,'z_far'=4,'z_near'=2,'core'=2] {'y_f..., dimensions={0} | all-to-all | bytes 1048576 | tf_op jit(solution)/shard_map/all_to_all | solution.py:123
  38.8 0.6 convolution_multiply_fusion
  39.5 13.9 %all_to_all.21 = f32[32,9,1,128]{3,2,1,0:T(1,128)S(1)} all-to-all(f32[32,9,1,128]{3,2,1,0:T(1,128)S(1)} %bitcast.21), channel_id=1, replica_groups=mesh['frame'=4,'y_far'=4,'y_near'=2,'z_far'=4,'z_near'=2,'core'=2] {'fra..., dimensions={0} | all-to-all | bytes 294912 | tf_op jit(solution)/shard_map/all_to_all | solution.py:123
  53.5 15.2 %all_to_all.22 = f32[16,9,1,128]{3,2,1,0:T(1,128)S(1)} all-to-all(f32[16,9,1,128]{3,2,1,0:T(1,128)S(1)} %bitcast.18), channel_id=1, replica_groups=mesh['frame'=4,'y_far'=4,'y_near'=2,'z_far'=4,'z_near'=2,'core'=2] {'y_f..., dimensions={0} | all-to-all | bytes 147456 | tf_op jit(solution)/shard_map/all_to_all | solution.py:123
  68.7 11.9 %all_to_all.23 = f32[32,9,1,128]{3,2,1,0:T(1,128)S(1)} all-to-all(f32[32,9,1,128]{3,2,1,0:T(1,128)S(1)} %bitcast.17), channel_id=1, replica_groups=mesh['frame'=4,'y_far'=4,'y_near'=2,'z_far'=4,'z_near'=2,'core'=2] {'fra..., dimensions={0} | all-to-all | bytes 294912 | tf_op jit(solution)/shard_map/all_to_all | solution.py:123
  80.6 6.7 %factor.1 = f32[256,256]{1,0:T(8,128)} custom-call(f32[288,128]{1,0:T(8,128)S(1)} %bitcast.15), custom_call_target="tpu_custom_call" | custom-call | tf_op jit(solution)/shard_map/factor/pallas_call | solution.py:113
  (5 shorter events, 0.1 us)
